TPU v7x, 32 devices: a whole 2x2x4 slice. The times are simulated.
32 devices in a mesh: rows: 8 (over z, y), vecs: 4 (over x, core).
Axes of the slice: x: 2, y: 2, z: 4, core: 2. Of those that a mesh axis runs over, the one named last changes fastest.
Arguments:
- vectors: bfloat16 [24576, 512], P('rows', 'vecs'), may hold values from -8 to 8
- node_mass: float32 [24576], P('rows'), may hold values from 0.5 to 2
- cable_stiff: float32 [24576], P('rows'), may hold values from 0.1 to 1
- cable_nodes: int32 [8, 4], P('rows'), may hold values from 1 to 1152, 2304 in all within a row
- deck_rigidity: float32 [], replicated, may hold values from 0.3 to 1
- anchor_rows: int32 [8, 8, 4], P('rows'), may hold values from 0 to 3072, as said below
- anchor_stiff: float32 [8, 8, 4], P('rows'), may hold values from 0.2 to 1, as said below
- cut_low: float32 [], replicated, may hold values from 1.5 to 2.5
- top_bound: float32 [], replicated, may hold values from 7 to 9
Outputs:
- basis: bfloat16 [24576, 512], P('rows', 'vecs')
Inputs may be any that keep to these rules, and one draw needn't show every extreme that they name: anchor_rows[r, q, s] is a node of partition r coupled through slot s to partition q, or 3072 where the slot is empty; slot s of r towards q is live exactly when slot s of q towards r is; live slots come first; no partition has live slots towards itself; a partition that is not a pylon partition has live slots only towards the partitions beside it in the cyclic order, which fill all 4 slots, and towards at most 4 pylon partitions; pylon partitions come in pairs half the cyclic order apart, and the two of a pair fill all 4 slots towards each other. anchor_stiff[r, q, s] equals anchor_stiff[q, r, s].
All inputs are finite; a program needn't handle non-finite values.
Results may differ from a plain program's by a relative error of at most 0.0072.
The roundings to bfloat16 on the way count: a program that leaves them out, or rounds other values in their place, can miss the bound.
Values may be sent and summed in bfloat16 or wider, within the bound.
A program may use at most 64 MiB of HBM per device.

v0:
```python
import jax
import jax.numpy as jnp
from jax import lax
from jax.sharding import PartitionSpec as P

CABLE_ROWS = 2304


def with_halo(block, sides, width):
    for axis, dim in sides:
        count = lax.axis_size(axis)
        forward = [(i, i + 1) for i in range(count - 1)]
        backward = [(target, source) for source, target in forward]
        low = lax.ppermute(
            lax.slice_in_dim(block, block.shape[dim] - width, None, axis=dim), axis, forward
        )
        high = lax.ppermute(lax.slice_in_dim(block, 0, width, axis=dim), axis, backward)
        block = jnp.concatenate([low, block, high], axis=dim)
    return block


def body(
    vectors,
    node_mass,
    cable_stiff,
    cable_nodes,
    deck_rigidity,
    anchor_rows,
    anchor_stiff,
    cut_low,
    top_bound,
):
    part_count = lax.axis_size("rows")
    my_index = lax.axis_index("rows")
    own_width = vectors.shape[1]
    cable_ends = jnp.cumsum(cable_nodes[0])
    positions = jnp.arange(CABLE_ROWS - 1, dtype=jnp.int32) + 1
    breaks = jnp.any(positions[:, None] == cable_ends[None, :], axis=1)
    cable_links = jnp.where(breaks, 0.0, cable_stiff[: CABLE_ROWS - 1])[:, None]
    left_open = jnp.where(my_index > 0, deck_rigidity, 0.0)
    right_open = jnp.where(my_index < part_count - 1, deck_rigidity, 0.0)
    slot_rows = anchor_rows[0]
    slot_stiff = anchor_stiff[0][:, :, None]
    flat_rows = slot_rows.reshape(-1)

    def apply_operator(values):
        cable_part = values[:CABLE_ROWS]
        deck_part = values[CABLE_ROWS:]
        cable_flux = cable_links * (cable_part[:-1] - cable_part[1:])
        cable_side = jnp.pad(cable_flux, ((0, 1), (0, 0))) - jnp.pad(cable_flux, ((1, 0), (0, 0)))
        outgoing = jnp.take(values, slot_rows, axis=0, mode="fill", fill_value=0.0)
        incoming = lax.all_to_all(
            outgoing.astype(jnp.bfloat16), "rows", split_axis=0, concat_axis=0, tiled=True
        ).astype(outgoing.dtype)
        padded = with_halo(deck_part.astype(jnp.bfloat16), (("rows", 0),), 1).astype(
            deck_part.dtype
        )
        before_row = padded[0]
        after_row = padded[-1]
        deck_flux = deck_rigidity * (deck_part[:-1] - deck_part[1:])
        first_flux = left_open * (before_row - deck_part[0])
        last_flux = right_open * (deck_part[-1] - after_row)
        deck_side = jnp.concatenate([deck_flux, last_flux[None, :]], axis=0) - jnp.concatenate(
            [first_flux[None, :], deck_flux], axis=0
        )
        anchor_force = (slot_stiff * (outgoing - incoming)).reshape(-1, values.shape[1])
        anchor_side = jnp.zeros_like(values).at[flat_rows].add(anchor_force, mode="drop")
        springs = jnp.concatenate([cable_side, deck_side], axis=0)
        return node_mass[:, None] * values + springs + anchor_side

    start_block = vectors.astype(jnp.float32)
    center = (top_bound + cut_low) * 0.5
    half_width = (top_bound - cut_low) * 0.5
    first_degree = (apply_operator(start_block) - center * start_block) / half_width
    second_degree = (
        2.0 * (apply_operator(first_degree) - center * first_degree) / half_width - start_block
    )
    filtered = second_degree.astype(jnp.bfloat16)
    columns = lax.all_gather(filtered, "vecs", axis=1, tiled=True)
    total_rows = filtered.shape[0] * part_count
    gram_whole = jnp.einsum("rb,rc->bc", columns, columns, preferred_element_type=jnp.float32)
    gram_matrix = lax.psum(gram_whole, "rows") / total_rows
    lower_factor = jnp.linalg.cholesky(gram_matrix)
    identity = jnp.eye(gram_matrix.shape[0], dtype=jnp.float32)
    inverse = jax.scipy.linalg.solve_triangular(lower_factor, identity, lower=True)
    factor = inverse.T.astype(jnp.bfloat16)
    own_factor = lax.dynamic_slice_in_dim(factor, lax.axis_index("vecs") * own_width, own_width, 1)
    return jnp.dot(columns, own_factor, preferred_element_type=jnp.float32).astype(jnp.bfloat16)


def solution(mesh):
    return jax.shard_map(
        body,
        mesh=mesh,
        in_specs=(
            P("rows", "vecs"),
            P("rows"),
            P("rows"),
            P("rows", None),
            P(),
            P("rows", None, None),
            P("rows", None, None),
            P(),
            P(),
        ),
        out_specs=P("rows", "vecs"),
        check_vma=False,
    )
```

profile of v0, /device:TPU:0, one launch (start us, length us, event | category | flops | bytes accessed | tf_op | source)
XLA Modules:
  0.0 327.3 jit_solution(2909291328228950229)
XLA Ops:
  6.5 0.7 fusion.50
  7.3 1.3 collective-permute-start.1
  8.6 5.5 %collective-permute-start = (bf16[1,128]{1,0:T(2,128)(2,1)S(1)}, bf16[1,128]{1,0:T(2,128)(2,1)S(1)}, u32[]{:S(2)}, u32[]{:S(2)}) collective-permute-start(bf16[1,128]{1,0:T(2,128)(2,1)S(1)} %get-tuple-element.32), channel_id=1, source_target_pairs={{0,4},{4,8},{8,12},{12,16},{16,20},{20,24},{24,28},{1,5},{5,9},{9,... | collective-permute-start | bytes 776 | tf_op jit(solution)/shard_map/ppermute | solution.py:14
  14.1 1.2 convert_element_type.44
  15.6 0.6 gather_fusion
  16.2 0.7 select_convert_fusion.1
  16.9 6.2 %all-to-all-start = ((bf16[8,4,128]{2,1,0:T(4,128)(2,1)}), bf16[8,4,128]{2,1,0:T(4,128)(2,1)S(1)}, u32[]{:S(2)}, u32[]{:S(2)}) async-start(bf16[8,4,128]{2,1,0:T(4,128)(2,1)} %select_convert_fusion.1), calls=%async_computation | async-start | bytes 16384 | tf_op jit(solution)/shard_map/all_to_all | solution.py:52
  25.6 0.4 fusion.1
  26.0 1.1 pad_subtract_fusion.1
  27.6 2.9 maximum_add_fusion
  30.6 3.3 scatter_fusion
  33.9 2.5 fusion.47
  36.5 1.4 fusion
  37.9 0.6 gather_fusion.1
  38.4 0.7 fusion.49
  39.2 1.3 collective-permute-start.3
  40.4 4.6 %collective-permute-start.2 = (bf16[1,128]{1,0:T(2,128)(2,1)S(1)}, bf16[1,128]{1,0:T(2,128)(2,1)S(1)}, u32[]{:S(2)}, u32[]{:S(2)}) collective-permute-start(bf16[1,128]{1,0:T(2,128)(2,1)S(1)} %get-tuple-element.30), channel_id=1, source_target_pairs={{0,4},{4,8},{8,12},{12,16},{16,20},{20,24},{24,28},{1,5},{5,9},{9,... | collective-permute-start | bytes 776 | tf_op jit(solution)/shard_map/ppermute | solution.py:14
  45.0 2.8 pad_subtract_fusion
  47.8 0.7 select_convert_fusion
  48.4 0.9 slice.253
  49.4 6.0 %all-to-all-start.1 = ((bf16[8,4,128]{2,1,0:T(4,128)(2,1)}), bf16[8,4,128]{2,1,0:T(4,128)(2,1)S(1)}, u32[]{:S(2)}, u32[]{:S(2)}) async-start(bf16[8,4,128]{2,1,0:T(4,128)(2,1)} %select_convert_fusion), calls=%async_computation.1 | async-start | bytes 16384 | tf_op jit(solution)/shard_map/all_to_all | solution.py:52
  55.5 2.9 maximum_add_fusion.1
  58.4 3.5 %all-to-all-done.1 = bf16[8,4,128]{2,1,0:T(4,128)(2,1)S(1)} async-done(((bf16[8,4,128]{2,1,0:T(4,128)(2,1)}), bf16[8,4,128]{2,1,0:T(4,128)(2,1)S(1)}, u32[]{:S(2)}, u32[]{:S(2)}) %all-to-all-start.1) | async-done | bytes 8224 | tf_op jit(solution)/shard_map/all_to_all | solution.py:52
  62.0 3.3 scatter_fusion.1
  65.3 2.6 subtract_convert_fusion
  67.9 0.5 all-reduce.7.cloned.1.call-start
  68.4 26.4 %all-gather.2.cloned.1.call-done = bf16[3072,512]{1,0:T(8,128)(2,1)} async-done(((bf16[3072,128]{1,0:T(8,128)(2,1)}), bf16[3072,512]{1,0:T(8,128)(2,1)}) %all-gather.2.cloned.1.call-update) | async-done | bytes 3145744 | tf_op jit(solution)/shard_map/all_gather | solution.py:79
  94.9 5.7 %fusion.54 = f32[512,512]{0,1:T(8,128)} fusion(bf16[3072,512]{1,0:T(8,128)(2,1)} %all-gather.2.cloned.1.call-done), kind=kOutput, calls=%fused_computation.131 | convolution fusion | flops 1610612736 | bytes 4194304 | tf_op jit(solution)/shard_map/rb,rc->bc/dot_general | solution.py:81
  100.7 1.1 fusion.13
  101.8 77.2 %all-reduce.7.cloned.1.call-done = f32[512,512]{0,1:T(8,128)} async-done(((f32[512,512]{0,1:T(8,128)}), f32[512,512]{0,1:T(8,128)}) %all-reduce.7.cloned.1.call-update) | async-done | bytes 1048592 | tf_op jit(solution)/shard_map/psum | solution.py:82
  179.0 1.3 broadcast_multiply_fusion
  180.3 0.3 copy.33
  180.6 0.9 copy-done.2
  181.8 11.7 %cholesky.104 = f32[128,128]{1,0:T(8,128)S(1)} custom-call(f32[128,128]{1,0:T(8,128)S(1)} %cholesky.266), custom_call_target="Cholesky" | custom-call | tf_op jit(solution)/shard_map/jit(cholesky)/cholesky | solution.py:83
  193.7 9.8 %custom-call.31 = f32[1,128,128]{1,2,0:T(8,128)S(1)} custom-call(f32[1,128,128]{2,1,0:T(8,128)S(1)} %get-tuple-element.43), custom_call_target="InvertDiagBlocksLowerTriangular" | custom-call | tf_op jit(solution)/shard_map/jit(cholesky)/cholesky | solution.py:83
  203.8 0.3 convolution_subtract_fusion.3
  204.1 11.9 %cholesky.217 = f32[128,128]{1,0:T(8,128)S(1)} custom-call(f32[128,128]{1,0:T(8,128)S(1)} %cholesky.270), custom_call_target="Cholesky" | custom-call | tf_op jit(solution)/shard_map/jit(cholesky)/cholesky | solution.py:83
  216.0 9.8 %custom-call.32 = f32[1,128,128]{1,2,0:T(8,128)S(1)} custom-call(f32[1,128,128]{2,1,0:T(8,128)S(1)} %get-tuple-element.40), custom_call_target="InvertDiagBlocksLowerTriangular" | custom-call | tf_op jit(solution)/shard_map/jit(cholesky)/cholesky | solution.py:83
  226.1 0.4 convolution_subtract_fusion.4
  226.5 11.7 %cholesky.238 = f32[128,128]{1,0:T(8,128)S(1)} custom-call(f32[128,128]{1,0:T(8,128)S(1)} %cholesky.275), custom_call_target="Cholesky" | custom-call | tf_op jit(solution)/shard_map/jit(cholesky)/cholesky | solution.py:83
  238.3 9.8 %custom-call.33 = f32[1,128,128]{1,2,0:T(8,128)S(1)} custom-call(f32[1,128,128]{2,1,0:T(8,128)S(1)} %get-tuple-element.37), custom_call_target="InvertDiagBlocksLowerTriangular" | custom-call | tf_op jit(solution)/shard_map/jit(cholesky)/cholesky | solution.py:83
  248.3 0.4 convolution_subtract_fusion.5
  248.7 11.9 %cholesky.255 = f32[128,128]{1,0:T(8,128)S(1)} custom-call(f32[128,128]{1,0:T(8,128)S(1)} %convolution_subtract_fusion.5), custom_call_target="Cholesky" | custom-call | tf_op jit(solution)/shard_map/jit(cholesky)/cholesky | solution.py:83
  260.6 0.6 compare_reduce_fusion.2
  261.3 0.6 compare_reduce_fusion.1
  261.9 0.7 compare_reduce_fusion.3
  265.1 9.7 %while.1 = (s32[]{:T(128)}, f32[512,512]{1,0:T(8,128)S(1)}, s32[4,2]{0,1:T(2,128)S(1)}, f32[4,128,128]{2,1,0:T(8,128)}, s32[]{:T(128)}) while((s32[]{:T(128)}, f32[512,512]{1,0:T(8,128)S(1)}, s32[4,2]{0,1:T(2,128)S(1)}, f32[4,128,128]{2,1,0:T(8,128)}, s32[]{:T(128)}) %tuple.36), condition=%wide.while_cond, body=%wide.while_body.sunk | while | flops 2 | bytes 132205 | solution.py:85
  265.2 0.5 fusion.64
  265.7 1.8 bitcast_dynamic-update-slice_fusion.2
  267.7 0.5 fusion.64
  268.2 1.8 bitcast_dynamic-update-slice_fusion.2
  270.1 0.5 fusion.64
  270.6 1.8 bitcast_dynamic-update-slice_fusion.2
  272.5 0.5 fusion.64
  273.0 1.8 bitcast_dynamic-update-slice_fusion.2
  274.9 40.1 %custom-call.34 = f32[4,128,128]{1,2,0:T(8,128)S(1)} custom-call(f32[4,128,128]{2,1,0:T(8,128)} %get-tuple-element.13), custom_call_target="InvertDiagBlocksLowerTriangular" | custom-call | tf_op jit(solution)/shard_map/jit(_solve_triangular)/triangular_solve | solution.py:85
  315.0 0.3 fusion.51
  315.4 0.4 convolution_subtract_fusion.1
  315.7 0.4 fusion.52
  316.2 0.4 convolution_subtract_fusion
  316.6 0.4 fusion.53
  317.0 0.6 convolution_subtract_fusion.2
  317.7 0.4 convolution_convert_fusion.1
  318.1 2.1 convolution_convert_fusion
  (70 shorter events, 3.4 us)
Async XLA Ops:
  6.5 8.8 %copy-start.5 = (s32[1,8,4]{1,2,0:T(4,128)S(1)}, s32[1,8,4]{1,2,0:T(4,128)}, u32[]{:S(2)}) copy-start(s32[1,8,4]{1,2,0:T(4,128)} %param.16) | copy-start | bytes 388
  7.3 20.0 %collective-permute-start.1 = (bf16[1,128]{1,0:T(2,128)(2,1)S(1)}, bf16[1,128]{1,0:T(2,128)(2,1)S(1)}, u32[]{:S(2)}, u32[]{:S(2)}) collective-permute-start(bf16[1,128]{1,0:T(2,128)(2,1)S(1)} %get-tuple-element.33), channel_id=1, source_target_pairs={{4,0},{8,4},{12,8},{16,12},{20,16},{24,20},{28,24},{5,1},{9,5},{13... | collective-permute-start | bytes 776 | tf_op jit(solution)/shard_map/ppermute | solution.py:17
  8.5 16.7 %copy-start.8 = (s32[1,4]{1,0:T(1,128)S(1)}, s32[1,4]{1,0:T(1,128)}, u32[]{:S(2)}) copy-start(s32[1,4]{1,0:T(1,128)} %param.14) | copy-start | bytes 52
  8.6 17.0 %copy-start.6 = (f32[3072]{0:T(1024)S(1)}, f32[3072]{0:T(1024)}, u32[]{:S(2)}) copy-start(f32[3072]{0:T(1024)} %param.13) | copy-start | bytes 36868
  8.6 18.7 %collective-permute-start = (bf16[1,128]{1,0:T(2,128)(2,1)S(1)}, bf16[1,128]{1,0:T(2,128)(2,1)S(1)}, u32[]{:S(2)}, u32[]{:S(2)}) collective-permute-start(bf16[1,128]{1,0:T(2,128)(2,1)S(1)} %get-tuple-element.32), channel_id=1, source_target_pairs={{0,4},{4,8},{8,12},{12,16},{16,20},{20,24},{24,28},{1,5},{5,9},{9,... | collective-permute-start | bytes 776 | tf_op jit(solution)/shard_map/ppermute | solution.py:14
  16.9 13.6 %all-to-all-start = ((bf16[8,4,128]{2,1,0:T(4,128)(2,1)}), bf16[8,4,128]{2,1,0:T(4,128)(2,1)S(1)}, u32[]{:S(2)}, u32[]{:S(2)}) async-start(bf16[8,4,128]{2,1,0:T(4,128)(2,1)} %select_convert_fusion.1), calls=%async_computation | async-start | bytes 16384 | tf_op jit(solution)/shard_map/all_to_all | solution.py:52
  25.9 1.3 copy-start.7
  25.9 1.4 slice-start
  26.0 1.6 copy-start
  26.0 1.6 copy-start.4
  39.2 16.3 %collective-permute-start.3 = (bf16[1,128]{1,0:T(2,128)(2,1)S(1)}, bf16[1,128]{1,0:T(2,128)(2,1)S(1)}, u32[]{:S(2)}, u32[]{:S(2)}) collective-permute-start(bf16[1,128]{1,0:T(2,128)(2,1)S(1)} %get-tuple-element.31), channel_id=1, source_target_pairs={{4,0},{8,4},{12,8},{16,12},{20,16},{24,20},{28,24},{5,1},{9,5},{13... | collective-permute-start | bytes 776 | tf_op jit(solution)/shard_map/ppermute | solution.py:17
  40.4 15.0 %collective-permute-start.2 = (bf16[1,128]{1,0:T(2,128)(2,1)S(1)}, bf16[1,128]{1,0:T(2,128)(2,1)S(1)}, u32[]{:S(2)}, u32[]{:S(2)}) collective-permute-start(bf16[1,128]{1,0:T(2,128)(2,1)S(1)} %get-tuple-element.30), channel_id=1, source_target_pairs={{0,4},{4,8},{8,12},{12,16},{16,20},{20,24},{24,28},{1,5},{5,9},{9,... | collective-permute-start | bytes 776 | tf_op jit(solution)/shard_map/ppermute | solution.py:14
  49.4 12.5 %all-to-all-start.1 = ((bf16[8,4,128]{2,1,0:T(4,128)(2,1)}), bf16[8,4,128]{2,1,0:T(4,128)(2,1)S(1)}, u32[]{:S(2)}, u32[]{:S(2)}) async-start(bf16[8,4,128]{2,1,0:T(4,128)(2,1)} %select_convert_fusion), calls=%async_computation.1 | async-start | bytes 16384 | tf_op jit(solution)/shard_map/all_to_all | solution.py:52
  55.4 39.5 %all-gather.2.cloned.1.call-start = ((), (), s32[]{:S(2)}) async-start(), calls=%async_computation.2 | async-start | bytes 3932160 | tf_op jit(solution)/shard_map/all_gather | solution.py:79
  67.9 111.0 %all-reduce.7.cloned.1.call-start = ((), (), s32[]{:S(2)}) async-start(), calls=%async_computation.3 | async-start | bytes 2097152 | tf_op jit(solution)/shard_map/psum | solution.py:82
  180.3 1.2 copy-start.2
  265.0 50.4 %copy-start.3 = (f32[512,512]{1,0:T(8,128)S(1)}, f32[512,512]{1,0:T(8,128)}, u32[]{:S(2)}) copy-start(f32[512,512]{1,0:T(8,128)} %fusion.13) | copy-start | bytes 3145732
  316.2 1.9 copy-start.1
Sparse Core Ops, SparseCore 0:
  68.1 26.7 all-gather.1
  100.7 78.1 all-reduce.6
where the time goes:
time: 332 us; the launch traced here: 327 us
  other arithmetic  148 us (45%)
  waiting for transfers between devices  107 us (32%)
  starting transfers between devices  25.4 us (8%)
  between operations  18.5 us (6%)
  local copies, waits for them, and re-layouts  15.4 us (5%)
  matrix products  12.6 us (4%)
    another operation x14, other arithmetic, body(): lower_factor = jnp.linalg.cholesky(gram_matrix)  78.7 us
    psum x1, waiting for transfers between devices, body(): gram_matrix = lax.psum(gram_whole, 'rows') / total_rows  77.2 us
    another operation x3, other arithmetic, body(): jax.scipy.linalg.solve_triangular(lower_factor, identity, lower=True)  40.3 us
    all_gather x1, waiting for transfers between devices, body(): columns = lax.all_gather(filtered, 'vecs', axis=1, tiled=True)  26.4 us
    all_to_all x2, starting transfers between devices, apply_operator(): lax.all_to_all(outgoing.astype(jnp.bfloat16), 'rows', split_axis=0, conca...  12.2 us
    ppermute x2, starting transfers between devices, with_halo(): lax.ppermute(lax.slice_in_dim(block, block.shape[dim] - width, None, axis...  10.1 us
    another operation x12, local copies, waits for them, and re-layouts  9.73 us
  transfers between devices with their start and end apart: 8, of which 3 were waited for; matrix products, arithmetic and copies ran while one was open for 5% of the time, Pallas kernels for 0%

commit v1 on v0

--- a/solution.py
+++ b/solution.py
@@ -4,6 +4,10 @@
 from jax.sharding import PartitionSpec as P
 
 CABLE_ROWS = 2304
+
+
+def array_replace(mine):
+    return jnp.sum(lax.all_gather(mine, "rows"), axis=0)
 
 
 def with_halo(block, sides, width):
@@ -79,7 +83,7 @@
     columns = lax.all_gather(filtered, "vecs", axis=1, tiled=True)
     total_rows = filtered.shape[0] * part_count
     gram_whole = jnp.einsum("rb,rc->bc", columns, columns, preferred_element_type=jnp.float32)
-    gram_matrix = lax.psum(gram_whole, "rows") / total_rows
+    gram_matrix = array_replace(gram_whole) / total_rows
     lower_factor = jnp.linalg.cholesky(gram_matrix)
     identity = jnp.eye(gram_matrix.shape[0], dtype=jnp.float32)
     inverse = jax.scipy.linalg.solve_triangular(lower_factor, identity, lower=True)

time: 332 us -> 382 us (1.15)
  waiting for transfers between devices: 107 us -> 153 us
  other arithmetic: 148 us -> 152 us
    all_gather x0 -> x1, waiting for transfers between devices: none -> 123 us  [array_replace(): return jnp.sum(lax.all_gather(mine, 'rows'), axis=0)]
    psum x1 -> x0, waiting for transfers between devices: 77.2 us -> none  [body(): gram_matrix = lax.psum(gram_whole, 'rows') / total_rows]
    reduce_sum x0 -> x1, other arithmetic: none -> 4.49 us  [array_replace(): return jnp.sum(lax.all_gather(mine, 'rows'), axis=0)]
  transfers between devices with their start and end apart: 8 -> 8, of which waited for: 3 -> 3; matrix products, arithmetic and copies ran while one was open for 5% -> 4% of each run, Pallas kernels for 0% -> 0%
where the time goes in v1:
time: 382 us; the launch traced here: 378 us
  waiting for transfers between devices  153 us (40%)
  other arithmetic  152 us (40%)
  starting transfers between devices  25.5 us (7%)
  between operations  18.7 us (5%)
  local copies, waits for them, and re-layouts  15.9 us (4%)
  matrix products  12.8 us (3%)
    all_gather x1, waiting for transfers between devices, array_replace(): return jnp.sum(lax.all_gather(mine, 'rows'), axis=0)  123 us
    another operation x14, other arithmetic, body(): lower_factor = jnp.linalg.cholesky(gram_matrix)  78.8 us
    another operation x3, other arithmetic, body(): jax.scipy.linalg.solve_triangular(lower_factor, identity, lower=True)  40.3 us
    all_gather x1, waiting for transfers between devices, body(): columns = lax.all_gather(filtered, 'vecs', axis=1, tiled=True)  26.4 us
    all_to_all x2, starting transfers between devices, apply_operator(): lax.all_to_all(outgoing.astype(jnp.bfloat16), 'rows', split_axis=0, conca...  13.6 us
    another operation x12, local copies, waits for them, and re-layouts  10.8 us
    ppermute x2, starting transfers between devices, with_halo(): lax.ppermute(lax.slice_in_dim(block, block.shape[dim] - width, None, axis...  8.8 us
  transfers between devices with their start and end apart: 8, of which 3 were waited for; matrix products, arithmetic and copies ran while one was open for 4% of the time, Pallas kernels for 0%

profile of v1, /device:TPU:0, one launch (start us, length us, event | category | flops | bytes accessed | tf_op | source)
XLA Modules:
  0.0 377.8 jit_solution(12636417391464473819)
XLA Ops:
  6.5 0.7 fusion.50
  7.3 4.9 %collective-permute-start = (bf16[1,128]{1,0:T(2,128)(2,1)S(1)}, bf16[1,128]{1,0:T(2,128)(2,1)S(1)}, u32[]{:S(2)}, u32[]{:S(2)}) collective-permute-start(bf16[1,128]{1,0:T(2,128)(2,1)S(1)} %get-tuple-element.32), channel_id=1, source_target_pairs={{0,4},{4,8},{8,12},{12,16},{16,20},{20,24},{24,28},{1,5},{5,9},{9,... | collective-permute-start | bytes 776 | tf_op jit(solution)/shard_map/ppermute | solution.py:18
  12.2 1.3 collective-permute-start.1
  13.5 1.2 convert_element_type.44
  15.0 0.6 gather_fusion
  15.6 0.7 select_convert_fusion.1
  16.3 7.0 %all-to-all-start = ((bf16[8,4,128]{2,1,0:T(4,128)(2,1)}), bf16[8,4,128]{2,1,0:T(4,128)(2,1)S(1)}, u32[]{:S(2)}, u32[]{:S(2)}) async-start(bf16[8,4,128]{2,1,0:T(4,128)(2,1)} %select_convert_fusion.1), calls=%async_computation | async-start | bytes 16384 | tf_op jit(solution)/shard_map/all_to_all | solution.py:56
  25.7 0.4 fusion.1
  26.1 1.1 pad_subtract_fusion.1
  27.7 2.9 maximum_add_fusion
  30.7 3.3 scatter_fusion
  34.0 2.5 fusion.47
  36.6 1.4 fusion
  37.9 0.6 gather_fusion.1
  38.5 0.7 fusion.49
  39.2 3.9 %collective-permute-start.2 = (bf16[1,128]{1,0:T(2,128)(2,1)S(1)}, bf16[1,128]{1,0:T(2,128)(2,1)S(1)}, u32[]{:S(2)}, u32[]{:S(2)}) collective-permute-start(bf16[1,128]{1,0:T(2,128)(2,1)S(1)} %get-tuple-element.30), channel_id=1, source_target_pairs={{0,4},{4,8},{8,12},{12,16},{16,20},{20,24},{24,28},{1,5},{5,9},{9,... | collective-permute-start | bytes 776 | tf_op jit(solution)/shard_map/ppermute | solution.py:18
  43.1 1.3 collective-permute-start.3
  44.4 2.8 pad_subtract_fusion
  47.2 0.7 select_convert_fusion
  47.9 0.9 slice.253
  48.8 6.6 %all-to-all-start.1 = ((bf16[8,4,128]{2,1,0:T(4,128)(2,1)}), bf16[8,4,128]{2,1,0:T(4,128)(2,1)S(1)}, u32[]{:S(2)}, u32[]{:S(2)}) async-start(bf16[8,4,128]{2,1,0:T(4,128)(2,1)} %select_convert_fusion), calls=%async_computation.1 | async-start | bytes 16384 | tf_op jit(solution)/shard_map/all_to_all | solution.py:56
  55.6 2.9 maximum_add_fusion.1
  58.5 3.5 all-to-all-done.1
  62.1 3.3 scatter_fusion.1
  65.3 2.6 subtract_convert_fusion
  68.0 0.5 all-gather.6.cloned.1.call-start
  68.5 26.4 %all-gather.4.cloned.1.call-done = bf16[3072,512]{1,0:T(8,128)(2,1)} async-done(((bf16[3072,128]{1,0:T(8,128)(2,1)}), bf16[3072,512]{1,0:T(8,128)(2,1)}) %all-gather.4.cloned.1.call-update) | async-done | bytes 3145744 | tf_op jit(solution)/shard_map/all_gather | solution.py:83
  94.9 5.8 %fusion.54 = f32[512,512]{1,0:T(8,128)} fusion(bf16[3072,512]{1,0:T(8,128)(2,1)} %all-gather.4.cloned.1.call-done), kind=kOutput, calls=%fused_computation.131 | convolution fusion | flops 1610612736 | bytes 4194304 | tf_op jit(solution)/shard_map/rb,rc->bc/dot_general | solution.py:85
  100.9 1.1 fusion.13
  102.0 123.4 %all-gather.6.cloned.1.call-done = f32[4096,512]{1,0:T(8,128)} async-done(((f32[512,512]{1,0:T(8,128)}), f32[4096,512]{1,0:T(8,128)}) %all-gather.6.cloned.1.call-update) | async-done | bytes 8388624 | tf_op jit(solution)/shard_map/all_gather | solution.py:10
  225.4 4.5 %reduce_sum.9 = f32[512,512]{1,0:T(8,128)S(1)} reduce(f32[8,512,512]{2,1,0:T(8,128)} %bitcast.71, f32[]{:T(128)} %constant.175.clone.1), dimensions={0}, to_apply=%region_4.6 | reduce | flops 1835008 | bytes 9437188 | tf_op jit(solution)/shard_map/reduce_sum | solution.py:10
  229.9 0.3 copy.38
  230.4 0.3 copy.39
  231.0 11.7 %cholesky.104 = f32[128,128]{1,0:T(8,128)S(1)} custom-call(f32[128,128]{1,0:T(8,128)S(1)} %cholesky.266), custom_call_target="Cholesky" | custom-call | tf_op jit(solution)/shard_map/jit(cholesky)/cholesky | solution.py:87
  242.9 9.8 %custom-call.31 = f32[1,128,128]{1,2,0:T(8,128)S(1)} custom-call(f32[1,128,128]{2,1,0:T(8,128)S(1)} %get-tuple-element.43), custom_call_target="InvertDiagBlocksLowerTriangular" | custom-call | tf_op jit(solution)/shard_map/jit(cholesky)/cholesky | solution.py:87
  253.0 0.3 convolution_subtract_fusion.3
  253.3 11.9 %cholesky.217 = f32[128,128]{1,0:T(8,128)S(1)} custom-call(f32[128,128]{1,0:T(8,128)S(1)} %cholesky.270), custom_call_target="Cholesky" | custom-call | tf_op jit(solution)/shard_map/jit(cholesky)/cholesky | solution.py:87
  265.2 9.8 %custom-call.32 = f32[1,128,128]{1,2,0:T(8,128)S(1)} custom-call(f32[1,128,128]{2,1,0:T(8,128)S(1)} %get-tuple-element.40), custom_call_target="InvertDiagBlocksLowerTriangular" | custom-call | tf_op jit(solution)/shard_map/jit(cholesky)/cholesky | solution.py:87
  275.3 0.4 convolution_subtract_fusion.4
  275.7 11.7 %cholesky.238 = f32[128,128]{1,0:T(8,128)S(1)} custom-call(f32[128,128]{1,0:T(8,128)S(1)} %cholesky.275), custom_call_target="Cholesky" | custom-call | tf_op jit(solution)/shard_map/jit(cholesky)/cholesky | solution.py:87
  287.5 0.7 compare_reduce_fusion.2
  288.2 9.8 %custom-call.33 = f32[1,128,128]{1,2,0:T(8,128)S(1)} custom-call(f32[1,128,128]{2,1,0:T(8,128)S(1)} %get-tuple-element.37), custom_call_target="InvertDiagBlocksLowerTriangular" | custom-call | tf_op jit(solution)/shard_map/jit(cholesky)/cholesky | solution.py:87
  298.2 0.4 convolution_subtract_fusion.5
  298.6 11.9 %cholesky.255 = f32[128,128]{1,0:T(8,128)S(1)} custom-call(f32[128,128]{1,0:T(8,128)S(1)} %convolution_subtract_fusion.5), custom_call_target="Cholesky" | custom-call | tf_op jit(solution)/shard_map/jit(cholesky)/cholesky | solution.py:87
  310.5 0.7 compare_reduce_fusion.1
  311.2 0.7 compare_reduce_fusion.3
  314.6 10.8 %while.1 = (s32[]{:T(128)}, f32[512,512]{1,0:T(8,128)S(1)}, s32[4,2]{0,1:T(2,128)S(1)}, f32[4,128,128]{2,1,0:T(8,128)}, s32[]{:T(128)}) while((s32[]{:T(128)}, f32[512,512]{1,0:T(8,128)S(1)}, s32[4,2]{0,1:T(2,128)S(1)}, f32[4,128,128]{2,1,0:T(8,128)}, s32[]{:T(128)}) %tuple.36), condition=%wide.while_cond, body=%wide.while_body.sunk | while | flops 2 | bytes 132705 | solution.py:89
  314.7 0.6 fusion.64
  315.3 2.0 bitcast_dynamic-update-slice_fusion.2
  317.4 0.6 fusion.64
  318.0 2.0 bitcast_dynamic-update-slice_fusion.2
  320.1 0.6 fusion.64
  320.7 2.0 bitcast_dynamic-update-slice_fusion.2
  322.8 0.6 fusion.64
  323.4 2.0 bitcast_dynamic-update-slice_fusion.2
  325.4 40.1 %custom-call.34 = f32[4,128,128]{1,2,0:T(8,128)S(1)} custom-call(f32[4,128,128]{2,1,0:T(8,128)} %get-tuple-element.13), custom_call_target="InvertDiagBlocksLowerTriangular" | custom-call | tf_op jit(solution)/shard_map/jit(_solve_triangular)/triangular_solve | solution.py:89
  365.6 0.3 fusion.51
  365.9 0.4 convolution_subtract_fusion.1
  366.3 0.4 fusion.52
  366.7 0.4 convolution_subtract_fusion
  367.1 0.4 fusion.53
  367.6 0.6 convolution_subtract_fusion.2
  368.2 0.4 convolution_convert_fusion.1
  368.7 2.1 convolution_convert_fusion
  (70 shorter events, 3.5 us)
Async XLA Ops:
  6.5 8.2 %copy-start.4 = (s32[1,8,4]{1,2,0:T(4,128)S(1)}, s32[1,8,4]{1,2,0:T(4,128)}, u32[]{:S(2)}) copy-start(s32[1,8,4]{1,2,0:T(4,128)} %param.16) | copy-start | bytes 388
  7.3 20.1 %collective-permute-start = (bf16[1,128]{1,0:T(2,128)(2,1)S(1)}, bf16[1,128]{1,0:T(2,128)(2,1)S(1)}, u32[]{:S(2)}, u32[]{:S(2)}) collective-permute-start(bf16[1,128]{1,0:T(2,128)(2,1)S(1)} %get-tuple-element.32), channel_id=1, source_target_pairs={{0,4},{4,8},{8,12},{12,16},{16,20},{20,24},{24,28},{1,5},{5,9},{9,... | collective-permute-start | bytes 776 | tf_op jit(solution)/shard_map/ppermute | solution.py:18
  12.1 13.2 %copy-start.7 = (s32[1,4]{1,0:T(1,128)S(1)}, s32[1,4]{1,0:T(1,128)}, u32[]{:S(2)}) copy-start(s32[1,4]{1,0:T(1,128)} %param.14) | copy-start | bytes 52
  12.2 13.5 %copy-start.5 = (f32[3072]{0:T(1024)S(1)}, f32[3072]{0:T(1024)}, u32[]{:S(2)}) copy-start(f32[3072]{0:T(1024)} %param.13) | copy-start | bytes 36868
  12.2 15.2 %collective-permute-start.1 = (bf16[1,128]{1,0:T(2,128)(2,1)S(1)}, bf16[1,128]{1,0:T(2,128)(2,1)S(1)}, u32[]{:S(2)}, u32[]{:S(2)}) collective-permute-start(bf16[1,128]{1,0:T(2,128)(2,1)S(1)} %get-tuple-element.33), channel_id=1, source_target_pairs={{4,0},{8,4},{12,8},{16,12},{20,16},{24,20},{28,24},{5,1},{9,5},{13... | collective-permute-start | bytes 776 | tf_op jit(solution)/shard_map/ppermute | solution.py:21
  16.3 14.3 %all-to-all-start = ((bf16[8,4,128]{2,1,0:T(4,128)(2,1)}), bf16[8,4,128]{2,1,0:T(4,128)(2,1)S(1)}, u32[]{:S(2)}, u32[]{:S(2)}) async-start(bf16[8,4,128]{2,1,0:T(4,128)(2,1)} %select_convert_fusion.1), calls=%async_computation | async-start | bytes 16384 | tf_op jit(solution)/shard_map/all_to_all | solution.py:56
  26.0 1.3 copy-start.6
  26.1 1.3 slice-start
  26.1 1.6 copy-start
  26.1 1.6 copy-start.3
  39.2 16.3 %collective-permute-start.2 = (bf16[1,128]{1,0:T(2,128)(2,1)S(1)}, bf16[1,128]{1,0:T(2,128)(2,1)S(1)}, u32[]{:S(2)}, u32[]{:S(2)}) collective-permute-start(bf16[1,128]{1,0:T(2,128)(2,1)S(1)} %get-tuple-element.30), channel_id=1, source_target_pairs={{0,4},{4,8},{8,12},{12,16},{16,20},{20,24},{24,28},{1,5},{5,9},{9,... | collective-permute-start | bytes 776 | tf_op jit(solution)/shard_map/ppermute | solution.py:18
  43.1 12.4 %collective-permute-start.3 = (bf16[1,128]{1,0:T(2,128)(2,1)S(1)}, bf16[1,128]{1,0:T(2,128)(2,1)S(1)}, u32[]{:S(2)}, u32[]{:S(2)}) collective-permute-start(bf16[1,128]{1,0:T(2,128)(2,1)S(1)} %get-tuple-element.31), channel_id=1, source_target_pairs={{4,0},{8,4},{12,8},{16,12},{20,16},{24,20},{28,24},{5,1},{9,5},{13... | collective-permute-start | bytes 776 | tf_op jit(solution)/shard_map/ppermute | solution.py:21
  48.8 13.2 %all-to-all-start.1 = ((bf16[8,4,128]{2,1,0:T(4,128)(2,1)}), bf16[8,4,128]{2,1,0:T(4,128)(2,1)S(1)}, u32[]{:S(2)}, u32[]{:S(2)}) async-start(bf16[8,4,128]{2,1,0:T(4,128)(2,1)} %select_convert_fusion), calls=%async_computation.1 | async-start | bytes 16384 | tf_op jit(solution)/shard_map/all_to_all | solution.py:56
  55.4 39.5 %all-gather.4.cloned.1.call-start = ((), (), s32[]{:S(2)}) async-start(), calls=%async_computation.2 | async-start | bytes 3932160 | tf_op jit(solution)/shard_map/all_gather | solution.py:83
  68.0 157.4 %all-gather.6.cloned.1.call-start = ((), (), s32[]{:S(2)}) async-start(), calls=%async_computation.3 | async-start | bytes 9437184 | tf_op jit(solution)/shard_map/all_gather | solution.py:10
  314.5 51.4 %copy-start.2 = (f32[512,512]{1,0:T(8,128)S(1)}, f32[512,512]{1,0:T(8,128)}, u32[]{:S(2)}) copy-start(f32[512,512]{1,0:T(8,128)} %fusion.13) | copy-start | bytes 3145732
  366.7 1.9 copy-start.1
Sparse Core Ops, SparseCore 0:
  68.1 26.7 all-gather.3
  100.9 124.4 all-gather.5
